TPU v7x, 128 devices: a whole 4x4x4 slice. The times are simulated.
128 devices in a mesh: band: 8 (over z_hi, y), lon: 16 (over z_lo, x, core).
Axes of the slice: x: 4, y: 4, z: 4 (z_hi: 2, z_lo: 2; z = z_hi * 2 + z_lo), core: 2. Of those that a mesh axis runs over, the one named last changes fastest.
Arguments:
- latent: bfloat16 [256, 2048, 256], P('band', 'lon'), may hold values from -6 to 6
- row_index: int32 [8, 16, 32], P('band', 'lon'), may hold values from 0 to 31
- interp_weights: bfloat16 [4096, 128, 128], P(('band', 'lon')), may hold values from -0.5 to 0.5
- observation_slot_index: int32 [4096, 128], P(('band', 'lon')), may hold values from 0 to 6
- counts: int32 [4096], P(('band', 'lon')), may hold values from 32 to 128
- targets: bfloat16 [4096, 128, 128], P(('band', 'lon')), may hold values from -6 to 6
- gain: float32 [256], replicated, may hold values from 0.5 to 1.5
- w_in: bfloat16 [256, 512], replicated, may hold values from -0.375 to 0.375
- w_out: bfloat16 [512, 256], replicated, may hold values from -0.25 to 0.25
- head: bfloat16 [256, 128], replicated, may hold values from -0.375 to 0.375
Outputs:
- grad_latent: float32 [256, 2048, 256], P('band', 'lon')
- grad_w_in: float32 [256, 512], replicated
- grad_w_out: float32 [512, 256], replicated
- grad_gain: float32 [256], replicated
- grad_head: float32 [256, 128], replicated
All inputs are finite; a program needn't handle non-finite values.
Results may differ from a plain program's by a relative error of at most 0.007.
Values may be sent and summed in bfloat16 or wider, within the bound.
No kernel may reach another device: no remote copies, remote signals or barrier semaphores. Data moves between devices by JAX's collectives and lax.ppermute only.
A program may use at most 128 MiB of HBM per device.

v0:
```python
import math
import jax
import jax.numpy as jnp
from jax import lax
from jax.sharding import PartitionSpec as P

WINDOW_SLOTS = 7
norm_eps = 1e-05


def padded_2(cells, sides, width):
    for axis, dim in sides:
        count = lax.axis_size(axis)
        head = lax.slice_in_dim(cells, 0, width, axis=dim)
        tail = lax.slice_in_dim(cells, cells.shape[dim] - width, cells.shape[dim], axis=dim)
        cells = jnp.concatenate(
            [
                lax.ppermute(tail, axis, [(i, (i + 1) % count) for i in range(count)]),
                cells,
                lax.ppermute(head, axis, [((i + 1) % count, i) for i in range(count)]),
            ],
            axis=dim,
        )
    return cells


def rounded_slots(values):
    return lax.optimization_barrier(values.astype(jnp.bfloat16))


def padded_mix(padded):
    return padded[:, 1:-1] + 0.5 * (padded[:, :-2] + padded[:, 2:])


def silu_slope(pre_act):
    sigmoid_a = jax.nn.sigmoid(pre_act)
    return sigmoid_a * (1.0 + pre_act * (1.0 - sigmoid_a))


def project_pair(weights, tile_pairs, temporal_weight, channels):
    proj_old = jnp.einsum(
        "bol,blc->boc", weights, tile_pairs[..., :channels], preferred_element_type=jnp.float32
    )
    proj_new = jnp.einsum(
        "bol,blc->boc", weights, tile_pairs[..., channels:], preferred_element_type=jnp.float32
    )
    return ((1.0 - temporal_weight) * proj_old + temporal_weight * proj_new).astype(jnp.bfloat16)


def pull_back(weights, obs_grad, temporal_weight):
    obs_float = obs_grad.astype(jnp.float32)
    back_old = ((1.0 - temporal_weight) * obs_float).astype(jnp.bfloat16)
    back_new = (temporal_weight * obs_float).astype(jnp.bfloat16)
    tile_old = jnp.einsum("bol,boc->blc", weights, back_old, preferred_element_type=jnp.float32)
    tile_new = jnp.einsum("bol,boc->blc", weights, back_new, preferred_element_type=jnp.float32)
    return jnp.concatenate([tile_old, tile_new], axis=-1).astype(jnp.bfloat16)


def decode(obs_latent, live_rows, goals, head, loss_scale):
    blocks, obs_rows, channels = obs_latent.shape
    flat_latent = obs_latent.reshape(-1, channels)
    predicted = jnp.dot(flat_latent, head, preferred_element_type=jnp.float32)
    residual = jnp.where(
        live_rows, predicted - goals.reshape(-1, head.shape[1]).astype(jnp.float32), 0.0
    )
    pred_grad = (residual * loss_scale).astype(jnp.bfloat16)
    head_grad = jnp.einsum("rc,rv->cv", flat_latent, pred_grad, preferred_element_type=jnp.float32)
    obs_grad = jnp.einsum("rv,cv->rc", pred_grad, head, preferred_element_type=jnp.float32).astype(
        jnp.bfloat16
    )
    return (head_grad, obs_grad.reshape(blocks, obs_rows, channels))


def body(
    latent,
    row_index,
    interp_weights,
    observation_slot_index,
    counts,
    targets,
    gain,
    w_in,
    w_out,
    head,
):
    lat_rows, lon_cells, channels = latent.shape
    peer_count = lax.axis_size("lon")
    devices_all = lax.axis_size("band") * peer_count
    blocks = interp_weights.shape[0]
    obs_rows = interp_weights.shape[1]
    per_peer = blocks // peer_count
    padded = padded_2(latent, (("lon", 1),), 1)
    summed = padded_mix(padded.astype(jnp.float32))
    inv_rms = lax.rsqrt(jnp.mean(summed * summed, axis=-1, keepdims=True) + norm_eps)
    normed = (summed * inv_rms * gain).astype(jnp.bfloat16)
    pre_act = jnp.einsum("lmc,ch->lmh", normed, w_in, preferred_element_type=jnp.float32)
    activated = jax.nn.silu(pre_act).astype(jnp.bfloat16)
    advanced = (
        latent.astype(jnp.float32)
        + jnp.einsum("lmh,hc->lmc", activated, w_out, preferred_element_type=jnp.float32)
    ).astype(jnp.bfloat16)
    stacked = jnp.concatenate([latent, advanced], axis=-1)
    requested = row_index.reshape(blocks)
    picked = stacked[requested]
    row_select = (requested[:, None] == jnp.arange(lat_rows, dtype=jnp.int32)[None, :]).astype(
        jnp.bfloat16
    )
    temporal_weight = rounded_slots(observation_slot_index.astype(jnp.float32) / (WINDOW_SLOTS - 1))
    live_flags = jnp.arange(obs_rows, dtype=jnp.int32)[None, :] < counts[:, None]
    live_rows = live_flags.reshape(-1, 1)
    loss_scale = 1.0 / math.sqrt(obs_rows)
    tile_pairs = lax.all_to_all(
        picked.reshape(peer_count, per_peer, lon_cells, 2 * channels),
        "lon",
        split_axis=0,
        concat_axis=0,
        tiled=True,
    )
    local_coef = temporal_weight.reshape(blocks, obs_rows, 1).astype(jnp.float32)
    obs_latent = project_pair(
        interp_weights, tile_pairs.reshape(blocks, lon_cells, 2 * channels), local_coef, channels
    )
    head_grad, obs_grad = decode(obs_latent, live_rows, targets, head, loss_scale)
    tile_grads = pull_back(interp_weights, obs_grad, local_coef)
    returned = lax.all_to_all(
        tile_grads.reshape(peer_count, per_peer, lon_cells, 2 * channels),
        "lon",
        split_axis=0,
        concat_axis=0,
        tiled=True,
    )
    grid_grad = jnp.einsum(
        "br,bx->rx",
        row_select,
        returned.reshape(blocks, lon_cells * 2 * channels),
        preferred_element_type=jnp.float32,
    )
    grid_grad = grid_grad.reshape(lat_rows, lon_cells, 2 * channels)
    grad_adv = grid_grad[..., channels:].astype(jnp.bfloat16)
    grad_out = jnp.einsum("lmh,lmc->hc", activated, grad_adv, preferred_element_type=jnp.float32)
    act_grad = jnp.einsum("lmc,hc->lmh", grad_adv, w_out, preferred_element_type=jnp.float32)
    pre_grad = (act_grad * silu_slope(pre_act)).astype(jnp.bfloat16)
    grad_in = jnp.einsum("lmc,lmh->ch", normed, pre_grad, preferred_element_type=jnp.float32)
    normed_grad = jnp.einsum("lmh,ch->lmc", pre_grad, w_in, preferred_element_type=jnp.float32)
    grad_gain = jnp.sum(normed_grad * summed * inv_rms, axis=(0, 1))
    gained = normed_grad * gain
    summed_grad = inv_rms * (
        gained - summed * inv_rms * inv_rms * jnp.mean(gained * summed, axis=-1, keepdims=True)
    )
    grad_padded = padded_2(summed_grad.astype(jnp.bfloat16), (("lon", 1),), 1).astype(
        summed_grad.dtype
    )
    grad_latent = grid_grad[..., :channels] + grid_grad[..., channels:] + padded_mix(grad_padded)
    totals = lax.psum((grad_in, grad_out, grad_gain, head_grad), ("band", "lon"))
    return (
        grad_latent,
        totals[0] / devices_all,
        totals[1] / devices_all,
        totals[2] / devices_all,
        totals[3] / devices_all,
    )


def solution(mesh):
    return jax.shard_map(
        body,
        mesh=mesh,
        in_specs=(
            P("band", "lon", None),
            P("band", "lon", None),
            P(("band", "lon"), None, None),
            P(("band", "lon"), None),
            P(("band", "lon")),
            P(("band", "lon"), None, None),
            P(),
            P(),
            P(),
            P(),
        ),
        out_specs=(P("band", "lon", None), P(), P(), P(), P()),
        check_vma=False,
    )
```

profile of v0, /device:TPU:1, one launch (start us, length us, event | category | flops | bytes accessed | tf_op | source)
XLA Modules:
  0.0 456.2 jit_solution(16606701495915434797)
XLA Ops:
  7.2 2.9 copy.28
  10.1 2.7 collective-permute-start
  13.6 2.6 collective-permute-done.1
  18.5 5.2 %multiply_convert_fusion.1 = (bf16[32,128,512]{2,1,0:T(8,128)(2,1)S(1)}, f32[32,128,512]{2,1,0:T(8,128)}) fusion(bf16[256,512]{1,0:T(8,128)(2,1)S(1)} %copy-done.21, bf16[32,128,256]{2,0,1:T(8,128)(2,1)S(1)} %multiply_convert_fusion.5), kind=kOutput, calls=%fused_computation.2 | convolution fusion | flops 1084227584 | bytes 14942208 | tf_op jit(solution)/shard_map/lmc,ch->lmh/dot_general | solution.py:96
  23.7 1.9 copy-done.10
  26.9 2.3 pad_maximum_fusion
  29.2 5.0 %gather_fusion = bf16[32,128,512]{2,1,0:T(8,128)(2,1)} fusion(bf16[32,128,512]{2,1,0:T(8,128)(2,1)} %pad_maximum_fusion, s32[1024]{0:T(1024)S(1)} %pad_clamp_fusion), kind=kCustom, calls=%fused_computation | custom fusion | bytes 8388736 | tf_op jit(solution)/shard_map/gather | solution.py:104
  34.2 6.4 %all-to-all-start = ((bf16[16,2,128,512]{3,2,1,0:T(8,128)(2,1)}), bf16[16,2,128,512]{3,2,1,0:T(8,128)(2,1)}, u32[]{:S(2)}, u32[]{:S(2)}) async-start(bf16[16,2,128,512]{3,2,1,0:T(8,128)(2,1)} %bitcast.68), calls=%async_computation | async-start | bytes 8388608 | tf_op jit(solution)/shard_map/all_to_all | solution.py:112
  40.8 56.3 %all-to-all-done = bf16[16,2,128,512]{3,2,1,0:T(8,128)(2,1)} async-done(((bf16[16,2,128,512]{3,2,1,0:T(8,128)(2,1)}), bf16[16,2,128,512]{3,2,1,0:T(8,128)(2,1)}, u32[]{:S(2)}, u32[]{:S(2)}) %all-to-all-start) | async-done | bytes 4194336 | tf_op jit(solution)/shard_map/all_to_all | solution.py:112
  97.0 2.3 fusion.18
  99.4 2.6 add_convert_fusion
  103.4 2.3 fusion.2
  107.4 3.4 copy.32
  110.9 3.0 fusion.24
  114.3 2.0 fusion.25
  116.3 3.9 copy.34
  120.3 2.6 copy.35
  122.8 4.6 %pad_maximum_fusion.1 = bf16[16,2,128,512]{3,2,1,0:T(8,128)(2,1)} fusion(bf16[16,2,128,256]{3,2,1,0:T(8,128)(2,1)} %copy.35, bf16[16,2,128,256]{3,2,1,0:T(8,128)(2,1)} %copy.34), kind=kLoop, calls=%fused_computation.21 | loop fusion | flops 8388608 | bytes 8388608 | tf_op jit(solution)/shard_map/concatenate | solution.py:56
  127.5 5.1 %all-to-all-start.1 = ((bf16[16,2,128,512]{3,2,1,0:T(8,128)(2,1)}), bf16[16,2,128,512]{3,2,1,0:T(8,128)(2,1)}, u32[]{:S(2)}, u32[]{:S(2)}) async-start(bf16[16,2,128,512]{3,2,1,0:T(8,128)(2,1)} %pad_maximum_fusion.1), calls=%async_computation.1 | async-start | bytes 8388608 | tf_op jit(solution)/shard_map/all_to_all | solution.py:125
  134.3 54.1 %all-to-all-done.1 = bf16[16,2,128,512]{3,2,1,0:T(8,128)(2,1)} async-done(((bf16[16,2,128,512]{3,2,1,0:T(8,128)(2,1)}), bf16[16,2,128,512]{3,2,1,0:T(8,128)(2,1)}, u32[]{:S(2)}, u32[]{:S(2)}) %all-to-all-start.1) | async-done | bytes 4194336 | tf_op jit(solution)/shard_map/all_to_all | solution.py:125
  188.4 5.4 %fusion.3 = f32[32,128,512]{2,0,1:T(8,128)S(1)} fusion(s32[32]{0:T(128)S(1)} %bitcast.74, bf16[4,8,128,512]{3,2,1,0:T(8,128)(2,1)} %bitcast.28), kind=kOutput, calls=%fused_computation.9 | convolution fusion | flops 134218752 | bytes 12583040 | tf_op jit(solution)/shard_map/br,bx->rx/dot_general | solution.py:132
  194.2 4.9 %copy-done.11 = bf16[32,128,512]{2,1,0:T(8,128)(2,1)S(1)} copy-done((bf16[32,128,512]{2,1,0:T(8,128)(2,1)S(1)}, bf16[32,128,512]{2,1,0:T(8,128)(2,1)}, u32[]{:S(2)}) %copy-start.11) | copy-done | bytes 4194328
  199.1 3.6 fusion.32
  202.6 6.6 %multiply_convert_fusion = bf16[32,128,512]{2,1,0:T(8,128)(2,1)S(1)} fusion(f32[32,128,512]{2,1,0:T(8,128)} %get-tuple-element.27, bf16[32,128,256]{2,0,1:T(8,128)(2,1)S(1)} %slice.98, bf16[512,256]{1,0:T(8,128)(2,1)S(1)} %copy-done.14), kind=kOutput, calls=%fused_computation.1 | convolution fusion | flops 1092616192 | bytes 14942208 | tf_op jit(solution)/shard_map/lmc,hc->lmh/dot_general | solution.py:141
  211.2 3.7 fusion.29
  214.8 8.9 %multiply_reduce_fusion = (f32[256]{0:T(256)S(1)}, f32[32,128]{0,1:T(8,128)S(1)}, f32[32,128,256]{2,0,1:T(8,128)}) fusion(f32[32,128,256]{2,0,1:T(8,128)} %copy-done.4, f32[32,128]{0,1:T(8,128)S(1)} %add_rsqrt_fusion, f32[256]{0:T(256)S(1)} %copy-done.17, bf16[256,512]{1,0:T(8,128)(2,1)S(1)} %copy-done.22, bf16[32,128,512]{2,1,0:T(8,128)(2,1)} %copy-done.23), kind=kOutput, calls=%fused_computation.22 | convolution fusion | flops 1080028928 | bytes 12879872 | tf_op jit(solution)/shard_map/lmh,ch->lmc/dot_general | solution.py:144
  223.7 67.3 %psum.30 = f32[256]{0:T(256)S(1)} all-reduce(f32[256]{0:T(256)S(1)} %get-tuple-element.15), channel_id=1, replica_groups=mesh['band'=8,'lon'=16] {'band','lon'}, use_global_device_ids=true, to_apply=%region_5.6 | all-reduce | flops 256 | bytes 2048 | tf_op jit(solution)/shard_map/psum | solution.py:154
  291.1 4.1 multiply_convert_fusion.2
  297.0 2.0 collective-permute-done.3
  299.4 5.1 %fusion.8 = f32[32,128,256]{2,0,1:T(8,128)S(1)} fusion(f32[32,130,256]{2,0,1:T(8,128)S(1)} %maximum_convert_fusion.1, f32[32,128,512]{2,0,1:T(8,128)} %copy-done.2), kind=kLoop, calls=%fused_computation.15 | loop fusion | flops 5242880 | bytes 25165824 | tf_op jit(solution)/shard_map/add | solution.py:153
  304.5 4.4 copy.43
  309.0 135.1 %all-reduce.3.cloned.1.call-done = (f32[256,512]{1,0:T(8,128)}, f32[512,256]{1,0:T(8,128)}, f32[256,128]{1,0:T(8,128)}) async-done(((f32[256,512]{1,0:T(8,128)}, f32[512,256]{1,0:T(8,128)}, f32[256,128]{1,0:T(8,128)}), (f32[256,512]{1,0:T(8,128)}, f32[512,256]{1,0:T(8,128)}, f32[256,128]{1,0:T(8,128)})) %all-reduce.3.cloned.1.call-update) | async-done | bytes 1179664 | tf_op jit(solution)/shard_map/psum | solution.py:154
  (75 shorter events, 19.5 us)
Async XLA Ops:
  7.2 89.9 %copy-start = (bf16[32,128,128]{2,1,0:T(8,128)(2,1)S(1)}, bf16[32,128,128]{2,1,0:T(8,128)(2,1)}, u32[]{:S(2)}) copy-start(bf16[32,128,128]{2,1,0:T(8,128)(2,1)} %param.12) | copy-start | bytes 3145732
  7.2 5.6 %copy-start.18 = (s32[1,1,32]{2,1,0:T(1,128)S(1)}, s32[1,1,32]{2,1,0:T(1,128)}, u32[]{:S(2)}) copy-start(s32[1,1,32]{2,1,0:T(1,128)} %param.11) | copy-start | bytes 388
  10.1 3.5 collective-permute-start
  12.7 3.5 collective-permute-start.1
  16.5 0.9 copy-start.17
  17.4 6.3 %copy-start.4 = (f32[32,128,256]{2,0,1:T(8,128)}, f32[32,128,256]{2,0,1:T(8,128)S(1)}, u32[]{:S(2)}) copy-start(f32[32,128,256]{2,0,1:T(8,128)S(1)} %get-tuple-element.21) | copy-start | bytes 12582916
  17.4 1.1 copy-start.21
  18.5 5.2 %copy-start.12 = (bf16[32,128,256]{2,0,1:T(8,128)(2,1)}, bf16[32,128,256]{2,0,1:T(8,128)(2,1)S(1)}, u32[]{:S(2)}) copy-start(bf16[32,128,256]{2,0,1:T(8,128)(2,1)S(1)} %multiply_convert_fusion.5) | copy-start | bytes 6291460
  18.5 7.1 %copy-start.5 = (bf16[32,128,256]{2,1,0:T(8,128)(2,1)S(1)}, bf16[32,128,256]{2,1,0:T(8,128)(2,1)}, u32[]{:S(2)}) copy-start(bf16[32,128,256]{2,1,0:T(8,128)(2,1)} %param.10) | copy-start | bytes 6291460
  18.5 7.1 %copy-start.14 = (bf16[512,256]{1,0:T(8,128)(2,1)S(1)}, bf16[512,256]{1,0:T(8,128)(2,1)}, u32[]{:S(2)}) copy-start(bf16[512,256]{1,0:T(8,128)(2,1)} %param.18) | copy-start | bytes 786436
  23.7 1.9 copy-start.10
  34.2 6.5 %copy-start.16 = (s32[32,128]{1,0:T(8,128)S(1)}, s32[32,128]{1,0:T(8,128)}, u32[]{:S(2)}) copy-start(s32[32,128]{1,0:T(8,128)} %param.13) | copy-start | bytes 49156
  34.2 6.5 %copy-start.19 = (s32[32]{0:T(128)S(1)}, s32[32]{0:T(128)}, u32[]{:S(2)}) copy-start(s32[32]{0:T(128)} %param.14) | copy-start | bytes 388
  34.2 62.8 %all-to-all-start = ((bf16[16,2,128,512]{3,2,1,0:T(8,128)(2,1)}), bf16[16,2,128,512]{3,2,1,0:T(8,128)(2,1)}, u32[]{:S(2)}, u32[]{:S(2)}) async-start(bf16[16,2,128,512]{3,2,1,0:T(8,128)(2,1)} %bitcast.68), calls=%async_computation | async-start | bytes 8388608 | tf_op jit(solution)/shard_map/all_to_all | solution.py:112
  99.3 4.1 copy-start.15
  99.3 4.1 copy-start.20
  102.0 1.4 copy-start.6
  105.7 1.1 copy-start.8
  110.9 3.4 copy-start.3
  127.5 5.4 %copy-start.7 = (bf16[32,256,128]{1,2,0:T(8,128)(2,1)S(1)}, bf16[32,256,128]{1,2,0:T(8,128)(2,1)}, u32[]{:S(2)}) copy-start(bf16[32,256,128]{1,2,0:T(8,128)(2,1)} %copy-done.6) | copy-start | bytes 6291460
  127.5 5.4 %copy-start.9 = (bf16[4096,128]{1,0:T(8,128)(2,1)S(1)}, bf16[4096,128]{1,0:T(8,128)(2,1)}, u32[]{:S(2)}) copy-start(bf16[4096,128]{1,0:T(8,128)(2,1)} %copy-done.8) | copy-start | bytes 3145732
  127.5 60.9 %all-to-all-start.1 = ((bf16[16,2,128,512]{3,2,1,0:T(8,128)(2,1)}), bf16[16,2,128,512]{3,2,1,0:T(8,128)(2,1)}, u32[]{:S(2)}, u32[]{:S(2)}) async-start(bf16[16,2,128,512]{3,2,1,0:T(8,128)(2,1)} %pad_maximum_fusion.1), calls=%async_computation.1 | async-start | bytes 8388608 | tf_op jit(solution)/shard_map/all_to_all | solution.py:125
  132.6 311.5 %all-reduce.3.cloned.1.call-start = ((), (), s32[]{:S(2)}) async-start(), calls=%async_computation.2 | async-start | bytes 2359296 | tf_op jit(solution)/shard_map/psum | solution.py:154
  193.8 8.8 %copy-start.2 = (f32[32,128,512]{2,0,1:T(8,128)}, f32[32,128,512]{2,0,1:T(8,128)S(1)}, u32[]{:S(2)}) copy-start(f32[32,128,512]{2,0,1:T(8,128)S(1)} %fusion.3) | copy-start | bytes 25165828
  193.8 5.2 %copy-start.11 = (bf16[32,128,512]{2,1,0:T(8,128)(2,1)S(1)}, bf16[32,128,512]{2,1,0:T(8,128)(2,1)}, u32[]{:S(2)}) copy-start(bf16[32,128,512]{2,1,0:T(8,128)(2,1)} %copy-done.10) | copy-start | bytes 12582916
  202.6 8.5 %copy-start.13 = (bf16[32,128,256]{2,0,1:T(8,128)(2,1)S(1)}, bf16[32,128,256]{2,0,1:T(8,128)(2,1)}, u32[]{:S(2)}) copy-start(bf16[32,128,256]{2,0,1:T(8,128)(2,1)} %copy-done.12) | copy-start | bytes 6291460
  209.2 2.0 copy-start.23
  211.1 3.7 copy-start.22
  295.2 1.8 collective-permute-start.2
  295.9 3.2 collective-permute-start.3
  299.4 150.0 %copy-start.1 = (bf16[32,128,128]{2,1,0:T(8,128)(2,1)S(1)}, bf16[32,128,128]{2,1,0:T(8,128)(2,1)}, u32[]{:S(2)}) copy-start(bf16[32,128,128]{2,1,0:T(8,128)(2,1)} %param.12) | copy-start | bytes 3145732
Sparse Core Ops, SparseCore 0:
  297.2 146.8 all-reduce.2
where the time goes:
time: 457 us; the launch traced here: 456 us
  waiting for transfers between devices  251 us (55%)
  blocking collectives  67.3 us (15%)
  matrix products  48.9 us (11%)
  local copies, waits for them, and re-layouts  34.6 us (8%)
  other arithmetic  24.4 us (5%)
  starting transfers between devices  15.7 us (3%)
  between operations  14.3 us (3%)
    psum x1, waiting for transfers between devices, body(): lax.psum((grad_in, grad_out, grad_gain, head_grad), ('band', 'lon'))  135 us
    psum x1, blocking collectives, body(): lax.psum((grad_in, grad_out, grad_gain, head_grad), ('band', 'lon'))  67.3 us
    all_to_all x1, waiting for transfers between devices, body(): lax.all_to_all(picked.reshape(peer_count, per_peer, lon_cells, 2 * channe...  56.3 us
    all_to_all x1, waiting for transfers between devices, body(): lax.all_to_all(tile_grads.reshape(peer_count, per_peer, lon_cells, 2 * ch...  54.1 us
    unnamed x50, local copies, waits for them, and re-layouts  19.3 us
  transfers between devices with their start and end apart: 7, of which 6 were waited for; matrix products, arithmetic and copies ran while one was open for 3% of the time, Pallas kernels for 0%

commit v1 on v0

--- a/solution.py
+++ b/solution.py
@@ -151,7 +151,7 @@
         summed_grad.dtype
     )
     grad_latent = grid_grad[..., :channels] + grid_grad[..., channels:] + padded_mix(grad_padded)
-    totals = lax.psum((grad_in, grad_out, grad_gain, head_grad), ("band", "lon"))
+    totals = lax.psum(lax.psum((grad_in, grad_out, grad_gain, head_grad), "band"), "lon")
     return (
         grad_latent,
         totals[0] / devices_all,

time: 457 us -> 439 us (0.961)
  blocking collectives: 67.3 us -> 50 us
  starting transfers between devices: 15.7 us -> 21.4 us
    psum x1 -> x2, blocking collectives: 67.3 us -> 50 us  [the longest x1 33 us: body(): lax.psum(lax.psum((grad_in, grad_out, grad_gain, head_grad), 'band'), 'lon')]
    ppermute x2, starting transfers between devices: 3.36 us -> 9.31 us  [padded_2(): lax.ppermute(tail, axis, [(i, (i + 1) % count) for i in range(count)])]
    psum x1 -> x2, waiting for transfers between devices: 135 us -> 135 us  [the longest x1 76 us: body(): lax.psum((grad_in, grad_out, grad_gain, head_grad), 'band')]
    unnamed x50 -> x52, local copies, waits for them, and re-layouts: 19.3 us -> 19.3 us
  transfers between devices with their start and end apart: 7 -> 8, of which waited for: 6 -> 6; matrix products, arithmetic and copies ran while one was open for 3% -> 5% of each run, Pallas kernels for 0% -> 0%
where the time goes in v1:
time: 439 us; the launch traced here: 438 us
  waiting for transfers between devices  249 us (57%)
  blocking collectives  50 us (11%)
  matrix products  47.2 us (11%)
  local copies, waits for them, and re-layouts  34.6 us (8%)
  other arithmetic  21.7 us (5%)
  starting transfers between devices  21.4 us (5%)
  between operations  14.4 us (3%)
    psum x1, waiting for transfers between devices, body(): lax.psum((grad_in, grad_out, grad_gain, head_grad), 'band')  76 us
    psum x1, waiting for transfers between devices, body(): lax.psum(lax.psum((grad_in, grad_out, grad_gain, head_grad), 'band'), 'lon')  59 us
    all_to_all x1, waiting for transfers between devices, body(): lax.all_to_all(picked.reshape(peer_count, per_peer, lon_cells, 2 * channe...  56.3 us
    all_to_all x1, waiting for transfers between devices, body(): lax.all_to_all(tile_grads.reshape(peer_count, per_peer, lon_cells, 2 * ch...  54.1 us
    psum x1, blocking collectives, body(): lax.psum(lax.psum((grad_in, grad_out, grad_gain, head_grad), 'band'), 'lon')  33 us
    unnamed x52, local copies, waits for them, and re-layouts  19.3 us
    psum x1, blocking collectives, body(): lax.psum((grad_in, grad_out, grad_gain, head_grad), 'band')  17 us
    ppermute x2, starting transfers between devices, padded_2(): lax.ppermute(tail, axis, [(i, (i + 1) % count) for i in range(count)])  9.31 us
  transfers between devices with their start and end apart: 8, of which 6 were waited for; matrix products, arithmetic and copies ran while one was open for 5% of the time, Pallas kernels for 0%

profile of v1, /device:TPU:1, one launch (start us, length us, event | category | flops | bytes accessed | tf_op | source)
XLA Modules:
  0.0 438.2 jit_solution(5191102673704235029)
XLA Ops:
  7.2 2.9 copy.28
  10.1 2.7 collective-permute-start
  13.6 2.6 collective-permute-done.1
  18.5 5.2 %multiply_convert_fusion.1 = (bf16[32,128,512]{2,1,0:T(8,128)(2,1)S(1)}, f32[32,128,512]{2,1,0:T(8,128)}) fusion(bf16[256,512]{1,0:T(8,128)(2,1)S(1)} %copy-done.22, bf16[32,128,256]{2,0,1:T(8,128)(2,1)S(1)} %multiply_convert_fusion.5), kind=kOutput, calls=%fused_computation.2 | convolution fusion | flops 1084227584 | bytes 14942208 | tf_op jit(solution)/shard_map/lmc,ch->lmh/dot_general | solution.py:96
  26.9 2.3 pad_maximum_fusion
  29.2 5.0 %gather_fusion = bf16[32,128,512]{2,1,0:T(8,128)(2,1)} fusion(bf16[32,128,512]{2,1,0:T(8,128)(2,1)} %pad_maximum_fusion, s32[1024]{0:T(1024)S(1)} %pad_clamp_fusion), kind=kCustom, calls=%fused_computation | custom fusion | bytes 8388736 | tf_op jit(solution)/shard_map/gather | solution.py:104
  34.2 6.4 %all-to-all-start = ((bf16[16,2,128,512]{3,2,1,0:T(8,128)(2,1)}), bf16[16,2,128,512]{3,2,1,0:T(8,128)(2,1)}, u32[]{:S(2)}, u32[]{:S(2)}) async-start(bf16[16,2,128,512]{3,2,1,0:T(8,128)(2,1)} %bitcast.68), calls=%async_computation | async-start | bytes 8388608 | tf_op jit(solution)/shard_map/all_to_all | solution.py:112
  40.8 56.3 %all-to-all-done = bf16[16,2,128,512]{3,2,1,0:T(8,128)(2,1)} async-done(((bf16[16,2,128,512]{3,2,1,0:T(8,128)(2,1)}), bf16[16,2,128,512]{3,2,1,0:T(8,128)(2,1)}, u32[]{:S(2)}, u32[]{:S(2)}) %all-to-all-start) | async-done | bytes 4194336 | tf_op jit(solution)/shard_map/all_to_all | solution.py:112
  97.0 2.3 fusion.18
  99.4 2.6 add_convert_fusion
  103.4 2.3 fusion.2
  107.4 3.4 copy.32
  110.9 3.0 fusion.24
  114.3 2.0 fusion.25
  116.3 3.9 copy.34
  120.3 2.6 copy.35
  122.8 4.6 %pad_maximum_fusion.1 = bf16[16,2,128,512]{3,2,1,0:T(8,128)(2,1)} fusion(bf16[16,2,128,256]{3,2,1,0:T(8,128)(2,1)} %copy.35, bf16[16,2,128,256]{3,2,1,0:T(8,128)(2,1)} %copy.34), kind=kLoop, calls=%fused_computation.21 | loop fusion | flops 8388608 | bytes 8388608 | tf_op jit(solution)/shard_map/concatenate | solution.py:56
  127.5 5.1 %all-to-all-start.1 = ((bf16[16,2,128,512]{3,2,1,0:T(8,128)(2,1)}), bf16[16,2,128,512]{3,2,1,0:T(8,128)(2,1)}, u32[]{:S(2)}, u32[]{:S(2)}) async-start(bf16[16,2,128,512]{3,2,1,0:T(8,128)(2,1)} %pad_maximum_fusion.1), calls=%async_computation.1 | async-start | bytes 8388608 | tf_op jit(solution)/shard_map/all_to_all | solution.py:125
  134.3 54.1 %all-to-all-done.1 = bf16[16,2,128,512]{3,2,1,0:T(8,128)(2,1)} async-done(((bf16[16,2,128,512]{3,2,1,0:T(8,128)(2,1)}), bf16[16,2,128,512]{3,2,1,0:T(8,128)(2,1)}, u32[]{:S(2)}, u32[]{:S(2)}) %all-to-all-start.1) | async-done | bytes 4194336 | tf_op jit(solution)/shard_map/all_to_all | solution.py:125
  188.4 5.4 %fusion.3 = f32[32,128,512]{2,0,1:T(8,128)S(1)} fusion(s32[32]{0:T(128)S(1)} %bitcast.74, bf16[4,8,128,512]{3,2,1,0:T(8,128)(2,1)} %bitcast.28), kind=kOutput, calls=%fused_computation.9 | convolution fusion | flops 134218752 | bytes 12583040 | tf_op jit(solution)/shard_map/br,bx->rx/dot_general | solution.py:132
  194.2 4.9 %copy-done.12 = bf16[32,128,512]{2,1,0:T(8,128)(2,1)S(1)} copy-done((bf16[32,128,512]{2,1,0:T(8,128)(2,1)S(1)}, bf16[32,128,512]{2,1,0:T(8,128)(2,1)}, u32[]{:S(2)}) %copy-start.12) | copy-done | bytes 4194328
  199.1 3.6 fusion.32
  202.6 6.6 %multiply_convert_fusion = bf16[32,128,512]{2,1,0:T(8,128)(2,1)S(1)} fusion(f32[32,128,512]{2,1,0:T(8,128)} %get-tuple-element.30, bf16[32,128,256]{2,0,1:T(8,128)(2,1)S(1)} %slice.98, bf16[512,256]{1,0:T(8,128)(2,1)S(1)} %copy-done.15), kind=kOutput, calls=%fused_computation.1 | convolution fusion | flops 1092616192 | bytes 14942208 | tf_op jit(solution)/shard_map/lmc,hc->lmh/dot_general | solution.py:141
  211.2 3.7 fusion.29
  215.2 7.2 %multiply_reduce_fusion = (f32[256]{0:T(256)S(1)}, f32[32,128]{0,1:T(8,128)S(1)}, f32[32,128,256]{2,0,1:T(8,128)S(1)}) fusion(f32[32,128,256]{2,0,1:T(8,128)} %copy-done.4, f32[32,128]{0,1:T(8,128)S(1)} %add_rsqrt_fusion, f32[256]{0:T(256)S(1)} %copy-done.18, bf16[256,512]{1,0:T(8,128)(2,1)S(1)} %copy-done.23, bf16[32,128,512]{2,1,0:T(8,128)(2,1)} %copy-done.24), kind=kOutput, calls=%fused_computation.22 | convolution fusion | flops 1080028928 | bytes 12879872 | tf_op jit(solution)/shard_map/lmh,ch->lmc/dot_general | solution.py:144
  224.1 76.0 %all-reduce.7.cloned.1.call-done = (f32[256,512]{1,0:T(8,128)}, f32[512,256]{1,0:T(8,128)}, f32[256,128]{1,0:T(8,128)}) async-done(((f32[256,512]{1,0:T(8,128)}, f32[512,256]{1,0:T(8,128)}, f32[256,128]{1,0:T(8,128)}), (f32[256,512]{1,0:T(8,128)}, f32[512,256]{1,0:T(8,128)}, f32[256,128]{1,0:T(8,128)})) %all-reduce.7.cloned.1.call-update) | async-done | bytes 1179664 | tf_op jit(solution)/shard_map/psum | solution.py:154
  300.1 6.6 %collective-permute-start.2 = (bf16[32,1,256]{2,0,1:T(8,128)(2,1)S(1)}, bf16[32,1,256]{2,0,1:T(8,128)(2,1)S(1)}, u32[]{:S(2)}, u32[]{:S(2)}) collective-permute-start(bf16[32,1,256]{2,0,1:T(8,128)(2,1)S(1)} %get-tuple-element.25), channel_id=1, source_target_pairs={{0,1},{1,2},{2,3},{3,4},{4,5},{5,6},{6,7},{7,8},{8,9},{9,10},{10,1... | collective-permute-start | bytes 49160 | tf_op jit(solution)/shard_map/ppermute | solution.py:18
  306.8 17.0 %psum.60 = f32[256]{0:T(256)S(1)} all-reduce(f32[256]{0:T(256)S(1)} %get-tuple-element.15), channel_id=1, replica_groups=mesh['band'=8,'lon'=16] {'band'}, use_global_device_ids=true, to_apply=%region_7.8 | all-reduce | flops 256 | bytes 2048 | tf_op jit(solution)/shard_map/psum | solution.py:154
  323.8 33.0 %psum.61 = f32[256]{0:T(256)S(1)} all-reduce(f32[256]{0:T(256)S(1)} %psum.60), channel_id=1, replica_groups=mesh['band'=8,'lon'=16] {'lon'}, use_global_device_ids=true, to_apply=%region_8.9 | all-reduce | flops 256 | bytes 2048 | tf_op jit(solution)/shard_map/psum | solution.py:154
  357.7 4.9 %fusion.8 = f32[32,128,256]{2,0,1:T(8,128)S(1)} fusion(f32[32,130,256]{2,0,1:T(8,128)S(1)} %maximum_convert_fusion.1, f32[32,128,512]{2,0,1:T(8,128)} %copy-done.2), kind=kLoop, calls=%fused_computation.15 | loop fusion | flops 5242880 | bytes 25165824 | tf_op jit(solution)/shard_map/add | solution.py:153
  362.6 4.4 %copy.43 = f32[32,128,256]{2,1,0:T(8,128)} copy(f32[32,128,256]{2,0,1:T(8,128)S(1)} %fusion.8) | data formatting | bytes 8388608
  367.1 59.0 %all-reduce.5.cloned.1.call-done = (f32[256,512]{1,0:T(8,128)}, f32[512,256]{1,0:T(8,128)}, f32[256,128]{1,0:T(8,128)}) async-done(((f32[256,512]{1,0:T(8,128)}, f32[512,256]{1,0:T(8,128)}, f32[256,128]{1,0:T(8,128)}), (f32[256,512]{1,0:T(8,128)}, f32[512,256]{1,0:T(8,128)}, f32[256,128]{1,0:T(8,128)})) %all-reduce.5.cloned.1.call-update) | async-done | bytes 1179664 | tf_op jit(solution)/shard_map/psum | solution.py:154
  (81 shorter events, 22.2 us)
Async XLA Ops:
  7.2 89.9 %copy-start = (bf16[32,128,128]{2,1,0:T(8,128)(2,1)S(1)}, bf16[32,128,128]{2,1,0:T(8,128)(2,1)}, u32[]{:S(2)}) copy-start(bf16[32,128,128]{2,1,0:T(8,128)(2,1)} %param.12) | copy-start | bytes 3145732
  7.2 5.6 %copy-start.19 = (s32[1,1,32]{2,1,0:T(1,128)S(1)}, s32[1,1,32]{2,1,0:T(1,128)}, u32[]{:S(2)}) copy-start(s32[1,1,32]{2,1,0:T(1,128)} %param.11) | copy-start | bytes 388
  10.1 3.5 collective-permute-start
  12.7 3.5 collective-permute-start.1
  17.4 6.3 %copy-start.4 = (f32[32,128,256]{2,0,1:T(8,128)}, f32[32,128,256]{2,0,1:T(8,128)S(1)}, u32[]{:S(2)}) copy-start(f32[32,128,256]{2,0,1:T(8,128)S(1)} %get-tuple-element.24) | copy-start | bytes 12582916
  17.4 1.1 copy-start.22
  18.5 5.2 %copy-start.13 = (bf16[32,128,256]{2,0,1:T(8,128)(2,1)}, bf16[32,128,256]{2,0,1:T(8,128)(2,1)S(1)}, u32[]{:S(2)}) copy-start(bf16[32,128,256]{2,0,1:T(8,128)(2,1)S(1)} %multiply_convert_fusion.5) | copy-start | bytes 6291460
  18.5 7.1 %copy-start.6 = (bf16[32,128,256]{2,1,0:T(8,128)(2,1)S(1)}, bf16[32,128,256]{2,1,0:T(8,128)(2,1)}, u32[]{:S(2)}) copy-start(bf16[32,128,256]{2,1,0:T(8,128)(2,1)} %param.10) | copy-start | bytes 6291460
  18.5 7.1 %copy-start.15 = (bf16[512,256]{1,0:T(8,128)(2,1)S(1)}, bf16[512,256]{1,0:T(8,128)(2,1)}, u32[]{:S(2)}) copy-start(bf16[512,256]{1,0:T(8,128)(2,1)} %param.18) | copy-start | bytes 786436
  23.7 1.9 copy-start.11
  34.2 6.5 %copy-start.17 = (s32[32,128]{1,0:T(8,128)S(1)}, s32[32,128]{1,0:T(8,128)}, u32[]{:S(2)}) copy-start(s32[32,128]{1,0:T(8,128)} %param.13) | copy-start | bytes 49156
  34.2 6.5 %copy-start.20 = (s32[32]{0:T(128)S(1)}, s32[32]{0:T(128)}, u32[]{:S(2)}) copy-start(s32[32]{0:T(128)} %param.14) | copy-start | bytes 388
  34.2 62.8 %all-to-all-start = ((bf16[16,2,128,512]{3,2,1,0:T(8,128)(2,1)}), bf16[16,2,128,512]{3,2,1,0:T(8,128)(2,1)}, u32[]{:S(2)}, u32[]{:S(2)}) async-start(bf16[16,2,128,512]{3,2,1,0:T(8,128)(2,1)} %bitcast.68), calls=%async_computation | async-start | bytes 8388608 | tf_op jit(solution)/shard_map/all_to_all | solution.py:112
  99.3 4.1 copy-start.16
  99.3 4.1 copy-start.21
  102.0 1.4 copy-start.7
  105.7 1.1 copy-start.9
  110.9 3.4 copy-start.3
  127.5 5.4 %copy-start.8 = (bf16[32,256,128]{1,2,0:T(8,128)(2,1)S(1)}, bf16[32,256,128]{1,2,0:T(8,128)(2,1)}, u32[]{:S(2)}) copy-start(bf16[32,256,128]{1,2,0:T(8,128)(2,1)} %copy-done.7) | copy-start | bytes 6291460
  127.5 5.4 %copy-start.10 = (bf16[4096,128]{1,0:T(8,128)(2,1)S(1)}, bf16[4096,128]{1,0:T(8,128)(2,1)}, u32[]{:S(2)}) copy-start(bf16[4096,128]{1,0:T(8,128)(2,1)} %copy-done.9) | copy-start | bytes 3145732
  127.5 60.9 %all-to-all-start.1 = ((bf16[16,2,128,512]{3,2,1,0:T(8,128)(2,1)}), bf16[16,2,128,512]{3,2,1,0:T(8,128)(2,1)}, u32[]{:S(2)}, u32[]{:S(2)}) async-start(bf16[16,2,128,512]{3,2,1,0:T(8,128)(2,1)} %pad_maximum_fusion.1), calls=%async_computation.1 | async-start | bytes 8388608 | tf_op jit(solution)/shard_map/all_to_all | solution.py:125
  132.6 167.5 %all-reduce.7.cloned.1.call-start = ((), (), s32[]{:S(2)}) async-start(), calls=%async_computation.3 | async-start | bytes 2359296 | tf_op jit(solution)/shard_map/psum | solution.py:154
  193.8 8.8 %copy-start.2 = (f32[32,128,512]{2,0,1:T(8,128)}, f32[32,128,512]{2,0,1:T(8,128)S(1)}, u32[]{:S(2)}) copy-start(f32[32,128,512]{2,0,1:T(8,128)S(1)} %fusion.3) | copy-start | bytes 25165828
  193.8 5.2 %copy-start.12 = (bf16[32,128,512]{2,1,0:T(8,128)(2,1)S(1)}, bf16[32,128,512]{2,1,0:T(8,128)(2,1)}, u32[]{:S(2)}) copy-start(bf16[32,128,512]{2,1,0:T(8,128)(2,1)} %copy-done.11) | copy-start | bytes 12582916
  202.6 8.5 %copy-start.14 = (bf16[32,128,256]{2,0,1:T(8,128)(2,1)S(1)}, bf16[32,128,256]{2,0,1:T(8,128)(2,1)}, u32[]{:S(2)}) copy-start(bf16[32,128,256]{2,0,1:T(8,128)(2,1)} %copy-done.13) | copy-start | bytes 6291460
  209.2 2.0 copy-start.24
  211.1 4.0 copy-start.23
  214.8 211.2 %all-reduce.5.cloned.1.call-start = ((), (), s32[]{:S(2)}) async-start(), calls=%async_computation.2 | async-start | bytes 2359296 | tf_op jit(solution)/shard_map/psum | solution.py:154
  215.2 7.3 %copy-start.5 = (f32[32,128,256]{2,0,1:T(8,128)S(1)}, f32[32,128,256]{2,0,1:T(8,128)}, u32[]{:S(2)}) copy-start(f32[32,128,256]{2,0,1:T(8,128)} %copy-done.4) | copy-start | bytes 12582916
  300.1 57.2 %collective-permute-start.2 = (bf16[32,1,256]{2,0,1:T(8,128)(2,1)S(1)}, bf16[32,1,256]{2,0,1:T(8,128)(2,1)S(1)}, u32[]{:S(2)}, u32[]{:S(2)}) collective-permute-start(bf16[32,1,256]{2,0,1:T(8,128)(2,1)S(1)} %get-tuple-element.25), channel_id=1, source_target_pairs={{0,1},{1,2},{2,3},{3,4},{4,5},{5,6},{6,7},{7,8},{8,9},{9,10},{10,1... | collective-permute-start | bytes 49160 | tf_op jit(solution)/shard_map/ppermute | solution.py:18
  306.7 50.6 %collective-permute-start.3 = (bf16[32,1,256]{2,0,1:T(8,128)(2,1)S(1)}, bf16[32,1,256]{2,0,1:T(8,128)(2,1)S(1)}, u32[]{:S(2)}, u32[]{:S(2)}) collective-permute-start(bf16[32,1,256]{2,0,1:T(8,128)(2,1)S(1)} %get-tuple-element.26), channel_id=1, source_target_pairs={{1,0},{2,1},{3,2},{4,3},{5,4},{6,5},{7,6},{8,7},{9,8},{10,9},{11,1... | collective-permute-start | bytes 49160 | tf_op jit(solution)/shard_map/ppermute | solution.py:20
  357.7 73.7 %copy-start.1 = (bf16[32,128,128]{2,1,0:T(8,128)(2,1)S(1)}, bf16[32,128,128]{2,1,0:T(8,128)(2,1)}, u32[]{:S(2)}) copy-start(bf16[32,128,128]{2,1,0:T(8,128)(2,1)} %param.12) | copy-start | bytes 3145732
  (1 other events, 0.9 us)
Sparse Core Ops, SparseCore 0:
  215.0 85.0 all-reduce.6
  302.8 123.2 all-reduce.4
